TPU v7x, 512 devices: a whole 4x4x16 slice. The times are simulated.
512 devices in a mesh: src: 16 (over z), tile: 8 (over x, core), gauge: 4 (over y).
Axes of the slice: x: 4, y: 4, z: 16, core: 2. Of those that a mesh axis runs over, the one named last changes fastest.
Arguments:
- responses: float32 [512, 2, 4, 128, 256], P(('src', 'tile'), None, 'gauge'), may hold values from -0.1875 to 0.1875
- footprint: int32 [512, 2], P(('src', 'tile')), may hold values from 0 to 15, all different within a row; in each aligned block of 4 rows (0 to 3, 4 to 7, ...) at most 2 rows name the same one
- theta_start: float32 [512, 8, 128], P(('src', 'tile')), may hold values from -4 to 4
- observed: float32 [128, 4, 8, 256], P(('src', 'tile'), 'gauge'), may hold values from -6 to 6
Outputs:
- theta: float32 [512, 8, 128], P(('src', 'tile'))
- misfit: float32 [128, 4, 8, 256], P(('src', 'tile'), 'gauge')
Inputs may be any that keep to these rules, and one draw needn't show every extreme that they name: `footprint`: each source's 2 entries differ. Among the 4 sources of one src and tile index, no value is named more than 2 times, a bound that some block reaches.
All inputs are finite; a program needn't handle non-finite values.
Results may differ from a plain program's by a relative error of at most 0.00017.
Values sent between devices are 32-bit elements; how exact they have to be, the bound alone decides.
A program may use at most 64 MiB of HBM per device.

v0:
```python
import jax
import jax.numpy as jnp
from jax import lax
from jax.sharding import PartitionSpec as P

GN_STEPS = 2
CG_ITERS = 2
damping = 0.1
highest = lax.Precision.HIGHEST


def local(responses, footprint, theta_start, observed):
    n_src = lax.axis_size("src")
    n_gauge = lax.axis_size("gauge")
    src_dev, foot, wins, width, length = responses.shape
    count = src_dev * foot
    blocks = responses.reshape(count, wins, width, length)
    target = footprint.reshape(count)
    dest_hot = (target[:, None] == jnp.arange(n_src, dtype=jnp.int32)[None, :]).astype(jnp.float32)
    capacity = max(2, -(-count // n_src))
    slots = n_src * capacity
    rank = jnp.sum(dest_hot * (jnp.cumsum(dest_hot, axis=0) - 1.0), axis=1).astype(jnp.int32)
    slot_of = target * capacity + rank
    slot_hot = (slot_of[:, None] == jnp.arange(slots, dtype=jnp.int32)[None, :]).astype(jnp.float32)
    observed_here = observed[0]
    packed_blocks = jnp.einsum("bq,bwkl->qwkl", slot_hot, blocks, precision=highest)
    received_blocks = lax.all_to_all(packed_blocks, "src", split_axis=0, concat_axis=0, tiled=True)

    def forward(values):
        spread = jnp.repeat(values, foot, axis=0)
        packed = jnp.einsum("bq,bek->qek", slot_hot, spread, precision=highest)
        arrived = lax.all_to_all(packed, "src", split_axis=0, concat_axis=0, tiled=True)
        return jnp.einsum("qek,qwkl->wel", arrived, received_blocks, precision=highest)

    def adjoint(field):
        backward = jnp.einsum("wel,qwkl->qek", field, received_blocks, precision=highest)
        returned = lax.all_to_all(backward, "src", split_axis=0, concat_axis=0, tiled=True)
        per_block = jnp.einsum("bq,qek->bek", slot_hot, returned, precision=highest)
        summed = jnp.sum(
            per_block.reshape(src_dev, foot, per_block.shape[1], per_block.shape[2]), axis=1
        )
        return lax.psum(summed, "gauge")

    theta = theta_start
    misfit = jnp.zeros_like(observed_here)
    for outer in range(GN_STEPS):
        coef = jax.nn.softplus(theta)
        slope = jax.nn.sigmoid(theta)
        misfit = forward(coef) - observed_here
        grad = slope * adjoint(misfit) + damping * theta
        update = jnp.zeros_like(theta)
        res = -grad
        direction = res
        norm_now = lax.psum(jnp.sum(res * res, axis=(0, 2)), ("src", "tile"))
        for inner in range(CG_ITERS):
            image = forward(slope * direction)
            norm_next = norm_now
            local_curv = (
                jnp.sum(image * image, axis=(0, 2))
                + damping * jnp.sum(direction * direction, axis=(0, 2)) / n_gauge
            )
            curv = lax.psum(local_curv, ("src", "tile", "gauge"))
            alpha = norm_now / curv
            applied = slope * adjoint(image) + damping * direction
            update = update + alpha[None, :, None] * direction
            res = res - alpha[None, :, None] * applied
            if inner + 1 < CG_ITERS:
                norm_next = lax.psum(jnp.sum(res * res, axis=(0, 2)), ("src", "tile"))
            if inner + 1 < CG_ITERS:
                direction = res + (norm_next / norm_now)[None, :, None] * direction
                norm_now = norm_next
        theta = theta + update
    return (theta, misfit[None])


def solution(mesh):
    in_specs = (
        P(("src", "tile"), None, "gauge", None, None),
        P(("src", "tile"), None),
        P(("src", "tile"), None, None),
        P(("src", "tile"), "gauge", None, None),
    )
    out_specs = (P(("src", "tile"), None, None), P(("src", "tile"), "gauge", None, None))
    return jax.shard_map(local, mesh=mesh, in_specs=in_specs, out_specs=out_specs, check_vma=False)
```

profile of v0, /device:TPU:1, one launch (start us, length us, event | category | flops | bytes accessed | tf_op | source)
XLA Modules:
  0.0 1926.5 jit_solution(504612940981126562)
XLA Ops:
  0.6 0.9 copy.83
  1.9 0.7 compare_select_fusion.1
  2.6 0.3 fusion.105
  3.0 0.7 copy.92
  3.7 15.7 all-to-all-start.1
  19.4 2.1 convolution_bitcast_fusion
  21.5 4.4 copy.85
  25.9 5.5 all-to-all-done.1
  31.4 6.7 all-to-all-start
  38.1 0.2 copy.93
  38.4 181.6 %all-to-all-done = f32[32,1,128,256]{3,2,1,0:T(8,128)} async-done(((f32[32,1,128,256]{3,2,1,0:T(8,128)}), f32[32,1,128,256]{3,2,1,0:T(8,128)}, u32[]{:S(2)}, u32[]{:S(2)}) %all-to-all-start) | async-done | bytes 4194336 | tf_op jit(solution)/shard_map/all_to_all | solution.py:27
  220.0 6.8 fusion.48
  226.8 12.1 fusion.30
  238.9 0.2 copy.94
  239.1 22.9 %all_to_all.55 = f32[32,8,128]{2,1,0:T(8,128)S(1)} all-to-all(f32[32,8,128]{2,1,0:T(8,128)S(1)} %copy.94), channel_id=1, replica_groups=mesh['src'=16,'tile'=8,'gauge'=4] {'src'}, dimensions={0} | all-to-all | bytes 262144 | tf_op jit(solution)/shard_map/all_to_all | solution.py:37
  262.0 0.2 fusion.82
  262.3 13.7 psum.84
  276.2 0.3 fusion.102
  276.6 18.1 all_to_all.56
  294.6 0.2 copy.98
  294.9 6.9 fusion.88
  301.8 12.1 fusion.33
  313.9 0.9 copy.99
  314.8 4.0 all-to-all-start.4
  318.8 252.9 %psum.85 = f32[8]{0:T(128)S(1)} all-reduce(f32[8]{0:T(128)S(1)} %get-tuple-element.16), channel_id=1, replica_groups=mesh['src'=16,'tile'=8,'gauge'=4] {'src','tile'}, use_global_device_ids=true, to_apply=%region_5.6 | all-reduce | flops 8 | bytes 64 | tf_op jit(solution)/shard_map/psum | solution.py:54
  571.7 99.7 %psum.86 = f32[8]{0:T(128)S(1)} all-reduce(f32[8]{0:T(128)S(1)} %multiply_add_fusion.7), channel_id=1, replica_groups=mesh['src'=16,'tile'=8,'gauge'=4] {'src','tile','gauge'}, use_global_device_ids=true, to_apply=%region_7.8 | all-reduce | flops 8 | bytes 64 | tf_op jit(solution)/shard_map/psum | solution.py:62
  671.4 0.2 fusion.80
  671.7 13.2 psum.87
  684.9 0.2 multiply_reduce_fusion.4
  685.1 250.6 %psum.88 = f32[8]{0:T(128)S(1)} all-reduce(f32[8]{0:T(128)S(1)} %get-tuple-element.14), channel_id=1, replica_groups=mesh['src'=16,'tile'=8,'gauge'=4] {'src','tile'}, use_global_device_ids=true, to_apply=%region_11.12 | all-reduce | flops 8 | bytes 64 | tf_op jit(solution)/shard_map/psum | solution.py:68
  935.7 0.2 multiply_reduce_fusion.3
  935.9 0.3 fusion.99
  936.3 22.0 %all_to_all.57 = f32[32,8,128]{2,1,0:T(8,128)S(1)} all-to-all(f32[32,8,128]{2,1,0:T(8,128)S(1)} %copy.101), channel_id=1, replica_groups=mesh['src'=16,'tile'=8,'gauge'=4] {'src'}, dimensions={0} | all-to-all | bytes 262144 | tf_op jit(solution)/shard_map/all_to_all | solution.py:32
  958.3 0.2 copy.102
  958.6 6.5 fusion.72
  965.1 101.3 %psum.89 = f32[8]{0:T(128)S(1)} all-reduce(f32[8]{0:T(128)S(1)} %multiply_add_fusion.6), channel_id=1, replica_groups=mesh['src'=16,'tile'=8,'gauge'=4] {'src','tile','gauge'}, use_global_device_ids=true, to_apply=%region_14.15 | all-reduce | flops 8 | bytes 64 | tf_op jit(solution)/shard_map/psum | solution.py:62
  1066.5 0.3 fusion.97
  1067.0 17.0 all_to_all.58
  1084.0 0.2 copy.105
  1084.3 6.8 fusion.60
  1091.1 12.1 fusion.36
  1103.2 0.2 copy.106
  1103.4 17.8 all_to_all.59
  1121.4 13.2 psum.90
  1134.8 0.3 fusion.94
  1135.2 17.3 all_to_all.60
  1152.6 0.2 copy.109
  1152.8 6.9 fusion.86
  1159.8 12.1 fusion.39
  1171.9 0.9 copy.110
  1172.7 4.0 all-to-all-start.9
  1176.7 253.3 %psum.91 = f32[8]{0:T(128)S(1)} all-reduce(f32[8]{0:T(128)S(1)} %get-tuple-element.10), channel_id=1, replica_groups=mesh['src'=16,'tile'=8,'gauge'=4] {'src','tile'}, use_global_device_ids=true, to_apply=%region_18.19 | all-reduce | flops 8 | bytes 64 | tf_op jit(solution)/shard_map/psum | solution.py:54
  1430.1 100.1 %psum.92 = f32[8]{0:T(128)S(1)} all-reduce(f32[8]{0:T(128)S(1)} %multiply_add_fusion.5), channel_id=1, replica_groups=mesh['src'=16,'tile'=8,'gauge'=4] {'src','tile','gauge'}, use_global_device_ids=true, to_apply=%region_20.21 | all-reduce | flops 8 | bytes 64 | tf_op jit(solution)/shard_map/psum | solution.py:62
  1530.2 0.2 fusion.76
  1530.5 13.2 psum.93
  1543.7 0.2 multiply_reduce_fusion.1
  1543.9 250.6 %psum.94 = f32[8]{0:T(128)S(1)} all-reduce(f32[8]{0:T(128)S(1)} %get-tuple-element.8), channel_id=1, replica_groups=mesh['src'=16,'tile'=8,'gauge'=4] {'src','tile'}, use_global_device_ids=true, to_apply=%region_24.25 | all-reduce | flops 8 | bytes 64 | tf_op jit(solution)/shard_map/psum | solution.py:68
  1794.5 0.2 multiply_reduce_fusion
  1794.7 0.3 fusion.91
  1795.1 22.1 %all_to_all.61 = f32[32,8,128]{2,1,0:T(8,128)S(1)} all-to-all(f32[32,8,128]{2,1,0:T(8,128)S(1)} %copy.112), channel_id=1, replica_groups=mesh['src'=16,'tile'=8,'gauge'=4] {'src'}, dimensions={0} | all-to-all | bytes 262144 | tf_op jit(solution)/shard_map/all_to_all | solution.py:32
  1817.2 0.2 copy.113
  1817.5 6.5 fusion.69
  1824.0 101.3 %psum.95 = f32[8]{0:T(128)S(1)} all-reduce(f32[8]{0:T(128)S(1)} %multiply_add_fusion.4), channel_id=1, replica_groups=mesh['src'=16,'tile'=8,'gauge'=4] {'src','tile','gauge'}, use_global_device_ids=true, to_apply=%region_27.28 | all-reduce | flops 8 | bytes 64 | tf_op jit(solution)/shard_map/psum | solution.py:62
  1925.4 0.6 copy.114
  (47 shorter events, 1.9 us)
Async XLA Ops:
  0.6 18.8 copy-start
  3.7 27.7 %all-to-all-start.1 = ((f32[32,8,128]{2,1,0:T(8,128)}), f32[32,8,128]{2,1,0:T(8,128)S(1)}, u32[]{:S(2)}, u32[]{:S(2)}) async-start(f32[32,8,128]{2,1,0:T(8,128)} %copy.92), calls=%async_computation.1 | async-start | bytes 262144 | tf_op jit(solution)/shard_map/all_to_all | solution.py:32
  25.9 194.0 %copy-start.2 = (f32[1,1,8,256]{3,2,1,0:T(8,128)S(1)}, f32[1,1,8,256]{3,2,1,0:T(8,128)}, u32[]{:S(2)}) copy-start(f32[1,1,8,256]{3,2,1,0:T(8,128)} %param.7) | copy-start | bytes 24580
  31.4 188.6 %all-to-all-start = ((f32[32,1,128,256]{3,2,1,0:T(8,128)}), f32[32,1,128,256]{3,2,1,0:T(8,128)}, u32[]{:S(2)}, u32[]{:S(2)}) async-start(f32[32,1,128,256]{3,2,1,0:T(8,128)} %copy.85), calls=%async_computation | async-start | bytes 8388608 | tf_op jit(solution)/shard_map/all_to_all | solution.py:27
  38.4 237.6 %copy-start.1 = (f32[4,8,128]{2,1,0:T(8,128)S(1)}, f32[4,8,128]{2,1,0:T(8,128)}, u32[]{:S(2)}) copy-start(f32[4,8,128]{2,1,0:T(8,128)} %param.6) | copy-start | bytes 49156
  314.8 356.6 %all-to-all-start.4 = ((f32[32,8,128]{2,1,0:T(8,128)}), f32[32,8,128]{2,1,0:T(8,128)S(1)}, u32[]{:S(2)}, u32[]{:S(2)}) async-start(f32[32,8,128]{2,1,0:T(8,128)} %copy.99), calls=%async_computation.4 | async-start | bytes 262144 | tf_op jit(solution)/shard_map/all_to_all | solution.py:37
  1091.1 68.7 %copy-start.3 = (f32[1,8,256]{2,1,0:T(8,128)}, f32[1,8,256]{2,1,0:T(8,128)S(1)}, u32[]{:S(2)}) copy-start(f32[1,8,256]{2,1,0:T(8,128)S(1)} %fusion.60) | copy-start | bytes 24580
  1172.7 357.5 %all-to-all-start.9 = ((f32[32,8,128]{2,1,0:T(8,128)}), f32[32,8,128]{2,1,0:T(8,128)S(1)}, u32[]{:S(2)}, u32[]{:S(2)}) async-start(f32[32,8,128]{2,1,0:T(8,128)} %copy.110), calls=%async_computation.9 | async-start | bytes 262144 | tf_op jit(solution)/shard_map/all_to_all | solution.py:37
where the time goes:
time: 1930 us
  blocking collectives  1600 us (83%)
  waiting for transfers between devices  187 us (10%)
  matrix products  93.6 us (5%)
  starting transfers between devices  30.5 us (2%)
    psum x2, blocking collectives, local(): norm_now = lax.psum(jnp.sum(res * res, axis=(0, 2)), ('src', 'tile'))  506 us
    psum x2, blocking collectives, local(): norm_next = lax.psum(jnp.sum(res * res, axis=(0, 2)), ('src', 'tile'))  501 us
    psum x4, blocking collectives, local(): curv = lax.psum(local_curv, ('src', 'tile', 'gauge'))  402 us
    all_to_all x1, waiting for transfers between devices, local(): lax.all_to_all(packed_blocks, 'src', split_axis=0, concat_axis=0, tiled=T...  182 us
    all_to_all x5, blocking collectives, forward(): lax.all_to_all(packed, 'src', split_axis=0, concat_axis=0, tiled=True)  96.6 us
    psum x4, blocking collectives, adjoint(): return lax.psum(summed, 'gauge')  53.3 us
    dot_general x4, matrix products, adjoint(): jnp.einsum('wel,qwkl->qek', field, received_blocks, precision=highest)  48.3 us
    all_to_all x2, blocking collectives, adjoint(): lax.all_to_all(backward, 'src', split_axis=0, concat_axis=0, tiled=True)  40.7 us
  transfers between devices with their start and end apart: 4, of which 2 were waited for; matrix products, arithmetic and copies ran while one was open for 0% of the time, Pallas kernels for 0%

commit v1 on v0

--- a/solution.py
+++ b/solution.py
@@ -51,7 +51,8 @@
         update = jnp.zeros_like(theta)
         res = -grad
         direction = res
-        norm_now = lax.psum(jnp.sum(res * res, axis=(0, 2)), ("src", "tile"))
+        one_axis = lax.psum(jnp.sum(res * res, axis=(0, 2)), "src")
+        norm_now = lax.psum(one_axis, "tile")
         for inner in range(CG_ITERS):
             image = forward(slope * direction)
             norm_next = norm_now

time: 1930 us -> 1520 us (0.79)
  blocking collectives: 1600 us -> 1190 us
    psum x2 -> x4, blocking collectives: 506 us -> 97.9 us  [the longest x2 49.8 us: local(): one_axis = lax.psum(jnp.sum(res * res, axis=(0, 2)), 'src')]
where the time goes in v1:
time: 1520 us; the launch traced here: 1510 us
  blocking collectives  1190 us (78%)
  waiting for transfers between devices  187 us (12%)
  matrix products  93.6 us (6%)
  starting transfers between devices  30.5 us (2%)
    psum x2, blocking collectives, local(): norm_next = lax.psum(jnp.sum(res * res, axis=(0, 2)), ('src', 'tile'))  501 us
    psum x4, blocking collectives, local(): curv = lax.psum(local_curv, ('src', 'tile', 'gauge'))  402 us
    all_to_all x1, waiting for transfers between devices, local(): lax.all_to_all(packed_blocks, 'src', split_axis=0, concat_axis=0, tiled=T...  182 us
    all_to_all x5, blocking collectives, forward(): lax.all_to_all(packed, 'src', split_axis=0, concat_axis=0, tiled=True)  93.9 us
    psum x4, blocking collectives, adjoint(): return lax.psum(summed, 'gauge')  50.2 us
    psum x2, blocking collectives, local(): one_axis = lax.psum(jnp.sum(res * res, axis=(0, 2)), 'src')  49.8 us
    dot_general x4, matrix products, adjoint(): jnp.einsum('wel,qwkl->qek', field, received_blocks, precision=highest)  48.3 us
    psum x2, blocking collectives, local(): norm_now = lax.psum(one_axis, 'tile')  48.1 us
  transfers between devices with their start and end apart: 4, of which 2 were waited for; matrix products, arithmetic and copies ran while one was open for 0% of the time, Pallas kernels for 0%

profile of v1, /device:TPU:1, one launch (start us, length us, event | category | flops | bytes accessed | tf_op | source)
XLA Modules:
  0.0 1512.1 jit_solution(8875483739247706153)
XLA Ops:
  0.6 0.9 copy.83
  1.9 0.7 compare_select_fusion.1
  2.6 0.3 fusion.105
  3.0 0.7 copy.92
  3.7 15.7 %all-to-all-start.1 = ((f32[32,8,128]{2,1,0:T(8,128)}), f32[32,8,128]{2,1,0:T(8,128)S(1)}, u32[]{:S(2)}, u32[]{:S(2)}) async-start(f32[32,8,128]{2,1,0:T(8,128)} %copy.92), calls=%async_computation.1 | async-start | bytes 262144 | tf_op jit(solution)/shard_map/all_to_all | solution.py:32
  19.4 2.1 convolution_bitcast_fusion
  21.5 4.4 copy.85
  25.9 5.5 all-to-all-done.1
  31.4 6.7 all-to-all-start
  38.1 0.2 copy.93
  38.4 181.6 %all-to-all-done = f32[32,1,128,256]{3,2,1,0:T(8,128)} async-done(((f32[32,1,128,256]{3,2,1,0:T(8,128)}), f32[32,1,128,256]{3,2,1,0:T(8,128)}, u32[]{:S(2)}, u32[]{:S(2)}) %all-to-all-start) | async-done | bytes 4194336 | tf_op jit(solution)/shard_map/all_to_all | solution.py:27
  220.0 6.8 fusion.48
  226.8 12.1 fusion.30
  238.9 0.2 copy.94
  239.1 22.9 %all_to_all.55 = f32[32,8,128]{2,1,0:T(8,128)S(1)} all-to-all(f32[32,8,128]{2,1,0:T(8,128)S(1)} %copy.94), channel_id=1, replica_groups=mesh['src'=16,'tile'=8,'gauge'=4] {'src'}, dimensions={0} | all-to-all | bytes 262144 | tf_op jit(solution)/shard_map/all_to_all | solution.py:37
  262.3 13.7 psum.98
  276.2 0.3 fusion.102
  276.6 18.1 %all_to_all.56 = f32[32,8,128]{2,1,0:T(8,128)S(1)} all-to-all(f32[32,8,128]{2,1,0:T(8,128)S(1)} %copy.97), channel_id=1, replica_groups=mesh['src'=16,'tile'=8,'gauge'=4] {'src'}, dimensions={0} | all-to-all | bytes 262144 | tf_op jit(solution)/shard_map/all_to_all | solution.py:32
  294.6 0.2 copy.98
  294.9 6.9 fusion.88
  301.8 12.1 fusion.33
  313.9 0.9 copy.99
  314.8 4.0 all-to-all-start.4
  318.8 25.1 %psum.99 = f32[8]{0:T(128)S(1)} all-reduce(f32[8]{0:T(128)S(1)} %get-tuple-element.16), channel_id=1, replica_groups=mesh['src'=16,'tile'=8,'gauge'=4] {'src'}, use_global_device_ids=true, to_apply=%region_5.6 | all-reduce | flops 8 | bytes 64 | tf_op jit(solution)/shard_map/psum | solution.py:54
  343.9 23.4 %psum.100 = f32[8]{0:T(128)S(1)} all-reduce(f32[8]{0:T(128)S(1)} %psum.99), channel_id=1, replica_groups=mesh['src'=16,'tile'=8,'gauge'=4] {'tile'}, use_global_device_ids=true, to_apply=%region_6.7 | all-reduce | flops 8 | bytes 64 | tf_op jit(solution)/shard_map/psum | solution.py:55
  367.3 99.8 %psum.101 = f32[8]{0:T(128)S(1)} all-reduce(f32[8]{0:T(128)S(1)} %multiply_add_fusion.7), channel_id=1, replica_groups=mesh['src'=16,'tile'=8,'gauge'=4] {'src','tile','gauge'}, use_global_device_ids=true, to_apply=%region_8.9 | all-reduce | flops 8 | bytes 64 | tf_op jit(solution)/shard_map/psum | solution.py:63
  467.1 0.2 fusion.80
  467.4 11.6 psum.102
  479.0 0.2 multiply_reduce_fusion.4
  479.2 250.6 %psum.103 = f32[8]{0:T(128)S(1)} all-reduce(f32[8]{0:T(128)S(1)} %get-tuple-element.14), channel_id=1, replica_groups=mesh['src'=16,'tile'=8,'gauge'=4] {'src','tile'}, use_global_device_ids=true, to_apply=%region_12.13 | all-reduce | flops 8 | bytes 64 | tf_op jit(solution)/shard_map/psum | solution.py:69
  729.8 0.2 multiply_reduce_fusion.3
  730.1 0.3 fusion.99
  730.5 20.7 %all_to_all.57 = f32[32,8,128]{2,1,0:T(8,128)S(1)} all-to-all(f32[32,8,128]{2,1,0:T(8,128)S(1)} %copy.101), channel_id=1, replica_groups=mesh['src'=16,'tile'=8,'gauge'=4] {'src'}, dimensions={0} | all-to-all | bytes 262144 | tf_op jit(solution)/shard_map/all_to_all | solution.py:32
  751.1 0.2 copy.102
  751.4 6.5 fusion.72
  757.9 101.3 %psum.104 = f32[8]{0:T(128)S(1)} all-reduce(f32[8]{0:T(128)S(1)} %multiply_add_fusion.6), channel_id=1, replica_groups=mesh['src'=16,'tile'=8,'gauge'=4] {'src','tile','gauge'}, use_global_device_ids=true, to_apply=%region_15.16 | all-reduce | flops 8 | bytes 64 | tf_op jit(solution)/shard_map/psum | solution.py:63
  859.3 0.3 fusion.97
  859.7 17.0 %all_to_all.58 = f32[32,8,128]{2,1,0:T(8,128)S(1)} all-to-all(f32[32,8,128]{2,1,0:T(8,128)S(1)} %copy.104), channel_id=1, replica_groups=mesh['src'=16,'tile'=8,'gauge'=4] {'src'}, dimensions={0} | all-to-all | bytes 262144 | tf_op jit(solution)/shard_map/all_to_all | solution.py:32
  876.8 0.2 copy.105
  877.0 6.8 fusion.60
  883.9 12.1 fusion.36
  895.9 0.2 copy.106
  896.2 17.8 %all_to_all.59 = f32[32,8,128]{2,1,0:T(8,128)S(1)} all-to-all(f32[32,8,128]{2,1,0:T(8,128)S(1)} %copy.106), channel_id=1, replica_groups=mesh['src'=16,'tile'=8,'gauge'=4] {'src'}, dimensions={0} | all-to-all | bytes 262144 | tf_op jit(solution)/shard_map/all_to_all | solution.py:37
  914.2 13.2 psum.105
  927.6 0.3 fusion.94
  928.0 17.3 %all_to_all.60 = f32[32,8,128]{2,1,0:T(8,128)S(1)} all-to-all(f32[32,8,128]{2,1,0:T(8,128)S(1)} %copy.108), channel_id=1, replica_groups=mesh['src'=16,'tile'=8,'gauge'=4] {'src'}, dimensions={0} | all-to-all | bytes 262144 | tf_op jit(solution)/shard_map/all_to_all | solution.py:32
  945.4 0.2 copy.109
  945.6 6.9 fusion.86
  952.6 12.1 fusion.39
  964.7 0.9 copy.110
  965.5 4.0 all-to-all-start.9
  969.5 24.7 %psum.106 = f32[8]{0:T(128)S(1)} all-reduce(f32[8]{0:T(128)S(1)} %get-tuple-element.10), channel_id=1, replica_groups=mesh['src'=16,'tile'=8,'gauge'=4] {'src'}, use_global_device_ids=true, to_apply=%region_19.20 | all-reduce | flops 8 | bytes 64 | tf_op jit(solution)/shard_map/psum | solution.py:54
  994.2 24.7 %psum.107 = f32[8]{0:T(128)S(1)} all-reduce(f32[8]{0:T(128)S(1)} %psum.106), channel_id=1, replica_groups=mesh['src'=16,'tile'=8,'gauge'=4] {'tile'}, use_global_device_ids=true, to_apply=%region_20.21 | all-reduce | flops 8 | bytes 64 | tf_op jit(solution)/shard_map/psum | solution.py:55
  1019.0 99.8 %psum.108 = f32[8]{0:T(128)S(1)} all-reduce(f32[8]{0:T(128)S(1)} %multiply_add_fusion.5), channel_id=1, replica_groups=mesh['src'=16,'tile'=8,'gauge'=4] {'src','tile','gauge'}, use_global_device_ids=true, to_apply=%region_22.23 | all-reduce | flops 8 | bytes 64 | tf_op jit(solution)/shard_map/psum | solution.py:63
  1119.0 11.6 psum.109
  1130.6 0.2 multiply_reduce_fusion.1
  1130.8 250.6 %psum.110 = f32[8]{0:T(128)S(1)} all-reduce(f32[8]{0:T(128)S(1)} %get-tuple-element.8), channel_id=1, replica_groups=mesh['src'=16,'tile'=8,'gauge'=4] {'src','tile'}, use_global_device_ids=true, to_apply=%region_26.27 | all-reduce | flops 8 | bytes 64 | tf_op jit(solution)/shard_map/psum | solution.py:69
  1381.4 0.2 multiply_reduce_fusion
  1381.7 0.3 fusion.91
  1382.1 20.7 %all_to_all.61 = f32[32,8,128]{2,1,0:T(8,128)S(1)} all-to-all(f32[32,8,128]{2,1,0:T(8,128)S(1)} %copy.112), channel_id=1, replica_groups=mesh['src'=16,'tile'=8,'gauge'=4] {'src'}, dimensions={0} | all-to-all | bytes 262144 | tf_op jit(solution)/shard_map/all_to_all | solution.py:32
  1402.8 0.2 copy.113
  1403.1 6.5 fusion.69
  1409.6 101.3 %psum.111 = f32[8]{0:T(128)S(1)} all-reduce(f32[8]{0:T(128)S(1)} %multiply_add_fusion.4), channel_id=1, replica_groups=mesh['src'=16,'tile'=8,'gauge'=4] {'src','tile','gauge'}, use_global_device_ids=true, to_apply=%region_29.30 | all-reduce | flops 8 | bytes 64 | tf_op jit(solution)/shard_map/psum | solution.py:63
  1511.0 0.6 copy.114
  (49 shorter events, 2.3 us)
Async XLA Ops:
  0.6 18.8 %copy-start = (f32[4,2,1,128,256]{4,3,2,1,0:T(8,128)S(1)}, f32[4,2,1,128,256]{4,3,2,1,0:T(8,128)}, u32[]{:S(2)}) copy-start(f32[4,2,1,128,256]{4,3,2,1,0:T(8,128)} %param.4) | copy-start | bytes 3145732
  3.7 27.7 %all-to-all-start.1 = ((f32[32,8,128]{2,1,0:T(8,128)}), f32[32,8,128]{2,1,0:T(8,128)S(1)}, u32[]{:S(2)}, u32[]{:S(2)}) async-start(f32[32,8,128]{2,1,0:T(8,128)} %copy.92), calls=%async_computation.1 | async-start | bytes 262144 | tf_op jit(solution)/shard_map/all_to_all | solution.py:32
  25.9 194.0 %copy-start.2 = (f32[1,1,8,256]{3,2,1,0:T(8,128)S(1)}, f32[1,1,8,256]{3,2,1,0:T(8,128)}, u32[]{:S(2)}) copy-start(f32[1,1,8,256]{3,2,1,0:T(8,128)} %param.7) | copy-start | bytes 24580
  31.4 188.6 %all-to-all-start = ((f32[32,1,128,256]{3,2,1,0:T(8,128)}), f32[32,1,128,256]{3,2,1,0:T(8,128)}, u32[]{:S(2)}, u32[]{:S(2)}) async-start(f32[32,1,128,256]{3,2,1,0:T(8,128)} %copy.85), calls=%async_computation | async-start | bytes 8388608 | tf_op jit(solution)/shard_map/all_to_all | solution.py:27
  38.4 237.6 %copy-start.1 = (f32[4,8,128]{2,1,0:T(8,128)S(1)}, f32[4,8,128]{2,1,0:T(8,128)}, u32[]{:S(2)}) copy-start(f32[4,8,128]{2,1,0:T(8,128)} %param.6) | copy-start | bytes 49156
  314.8 152.3 %all-to-all-start.4 = ((f32[32,8,128]{2,1,0:T(8,128)}), f32[32,8,128]{2,1,0:T(8,128)S(1)}, u32[]{:S(2)}, u32[]{:S(2)}) async-start(f32[32,8,128]{2,1,0:T(8,128)} %copy.99), calls=%async_computation.4 | async-start | bytes 262144 | tf_op jit(solution)/shard_map/all_to_all | solution.py:37
  883.8 68.7 %copy-start.3 = (f32[1,8,256]{2,1,0:T(8,128)}, f32[1,8,256]{2,1,0:T(8,128)S(1)}, u32[]{:S(2)}) copy-start(f32[1,8,256]{2,1,0:T(8,128)S(1)} %fusion.60) | copy-start | bytes 24580
  965.5 153.2 %all-to-all-start.9 = ((f32[32,8,128]{2,1,0:T(8,128)}), f32[32,8,128]{2,1,0:T(8,128)S(1)}, u32[]{:S(2)}, u32[]{:S(2)}) async-start(f32[32,8,128]{2,1,0:T(8,128)} %copy.110), calls=%async_computation.9 | async-start | bytes 262144 | tf_op jit(solution)/shard_map/all_to_all | solution.py:37
